TPU v7x, 32 devices: a whole 2x2x4 slice. The times are simulated.
32 devices in a mesh: dom: 16 (over z, y, x), row: 2 (over core).
Axes of the slice: x: 2, y: 2, z: 4, core: 2. Of those that a mesh axis runs over, the one named last changes fastest.
Arguments:
- features: float32 [4096, 128], P(('dom', 'row')), may hold values from -6 to 6
- history: float32 [4096, 1024], P(('dom', 'row')), may hold values from -3 to 3
- tiles: float32 [32, 4, 128, 128], P(('dom', 'row')), may hold values from -0.25 to 0.25
- tile_cols: int32 [32, 4], P(('dom', 'row')), may hold values from 0 to 1
- cross_weight: float32 [4096, 128], P(('dom', 'row')), may hold values from -0.75 to 0.75
- send_rows: int32 [32, 16, 8], P(('dom', 'row')), may hold values from 0 to 127
- send_count: int32 [32, 16], P(('dom', 'row')), may hold values from 0 to 8, as said below
- cotangent: float32 [4096, 172], P(('dom', 'row')), may hold values from -0.0234375 to 0.0234375
- w_one: float32 [128, 1024], replicated, may hold values from -0.5 to 0.5
- w_two: float32 [1024, 172], replicated, may hold values from -0.1875 to 0.1875
Outputs:
- logits: float32 [4096, 172], P(('dom', 'row'))
- grad_w1: float32 [128, 1024], replicated
- grad_w2: float32 [1024, 172], replicated
Inputs may be any that keep to these rules, and one draw needn't show every extreme that they name: send_count is 0 toward the sender's own partition; in every draw some partition receives 8 live rows from every device of every other partition.
All inputs are finite; a program needn't handle non-finite values.
Results may differ from a plain program's by a relative error of at most 0.0003.
Values sent between devices are 32-bit elements; how exact they have to be, the bound alone decides.
A program may use at most 64 MiB of HBM per device.

v0:
```python
import jax
import jax.numpy as jnp
from jax import lax
from jax.sharding import PartitionSpec as P

HIGH = lax.Precision.HIGHEST


def gate_act(values):
    sigma = jax.nn.sigmoid(values)
    return (values * sigma, sigma * (1.0 + values * (1.0 - sigma)))


def matmul(left, right):
    return jnp.dot(left, right, precision=HIGH, preferred_element_type=jnp.float32)


def on_device(
    features,
    history,
    tiles,
    tile_cols,
    cross_weight,
    send_rows,
    send_count,
    cotangent,
    w_one,
    w_two,
):
    rows_here = features.shape[0]
    blocks_here = tiles.shape[0]
    parts_count = send_rows.shape[1]
    slot_count = send_rows.shape[2]
    width_in = features.shape[1]
    width_hidden = history.shape[1]
    width_out = w_two.shape[1]
    lane_index = jnp.arange(128, dtype=jnp.int32)
    targets = tile_cols[:, :, None] * 128 + lane_index[None, None, :]
    live_mask = (jnp.arange(slot_count, dtype=jnp.int32)[None, :] < send_count[0][:, None]).astype(
        jnp.float32
    )
    pick_rows = send_rows[0]
    feat_out = jnp.take(features, pick_rows, axis=0) * live_mask[:, :, None]
    hist_out = jnp.take(history, pick_rows, axis=0) * live_mask[:, :, None]
    got_feat, got_hist = (
        lax.all_to_all(feat_out, "dom", split_axis=0, concat_axis=0, tiled=True),
        lax.all_to_all(hist_out, "dom", split_axis=0, concat_axis=0, tiled=True),
    )
    cross_feat = matmul(cross_weight, got_feat.reshape(parts_count * slot_count, width_in))
    cross_hist = matmul(cross_weight, got_hist.reshape(parts_count * slot_count, width_hidden))
    cross_logits = matmul(cross_hist, w_two)

    def add_panel(panel):
        row_count = panel.shape[0]
        inside = (targets >= 0) & (targets < row_count)
        picked = jnp.take(panel, jnp.clip(targets, 0, row_count - 1), axis=0)
        picked = picked * inside[..., None].astype(panel.dtype)
        return jnp.einsum("bkij,bkjw->biw", tiles, picked, precision=HIGH)

    local_feat = add_panel(lax.all_gather(features, "row", axis=0, tiled=True))
    layer_in = local_feat.reshape(rows_here, width_in) + cross_feat
    pre_act = matmul(layer_in, w_one)
    hidden, slope_gate = gate_act(pre_act)
    projected = matmul(hidden, w_two)
    local_out = add_panel(lax.all_gather(projected, "row", axis=0, tiled=True))
    logits = local_out.reshape(rows_here, width_out) + cross_logits
    blocked_grads = cotangent.reshape(blocks_here, 128, width_out)
    contrib = jnp.einsum("bkij,biw->bkjw", tiles, blocked_grads, precision=HIGH)
    block_ids = jnp.arange(lax.axis_size("row") * rows_here // 128, dtype=jnp.int32)
    hot = (tile_cols[:, :, None] == block_ids[None, None, :]).astype(jnp.float32)
    summed = jnp.einsum("bkc,bkjw->cjw", hot, contrib, precision=HIGH)
    back_grad = lax.psum_scatter(
        summed.reshape(lax.axis_size("row") * rows_here // 128 * 128, width_out),
        "row",
        scatter_dimension=0,
        tiled=True,
    )
    grad_two = matmul(hidden.T, back_grad)
    grad_two = grad_two + matmul(cross_hist.T, cotangent)
    grad_pre = matmul(back_grad, w_two.T) * slope_gate
    grad_one = matmul(layer_in.T, grad_pre)
    grad_one, grad_two = lax.psum((grad_one, grad_two), ("dom", "row"))
    return (logits, grad_one, grad_two)


def solution(mesh):
    placed = (
        P(("dom", "row"), None),
        P(("dom", "row"), None),
        P(("dom", "row"), None, None, None),
        P(("dom", "row"), None),
        P(("dom", "row"), None),
        P(("dom", "row"), None, None),
        P(("dom", "row"), None),
        P(("dom", "row"), None),
        P(),
        P(),
    )
    return jax.shard_map(
        on_device,
        mesh=mesh,
        in_specs=placed,
        out_specs=(P(("dom", "row"), None), P(), P()),
        check_vma=False,
    )
```

profile of v0, /device:TPU:0, one launch (start us, length us, event | category | flops | bytes accessed | tf_op | source)
XLA Modules:
  0.0 193.7 jit_solution(11159465152291520125)
XLA Ops:
  7.2 0.0 copy-start
  7.2 0.0 copy-start.10
  7.2 0.8 compare_and_fusion
  8.0 0.1 copy.20
  8.1 0.1 copy.21
  8.1 0.1 reshape.276
  8.2 0.0 copy-start.12
  8.2 0.6 copy-done.12
  8.9 0.1 fusion.26
  9.0 1.5 gather_fusion.1
  10.5 0.7 fusion.25
  11.2 8.3 %all-to-all-start = ((f32[16,8,128]{2,1,0:T(8,128)}), f32[16,8,128]{2,1,0:T(8,128)S(1)}, u32[]{:S(2)}, u32[]{:S(2)}) async-start(f32[16,8,128]{2,1,0:T(8,128)} %fusion.25), calls=%async_computation | async-start | bytes 131072 | tf_op jit(solution)/shard_map/all_to_all | solution.py:46
  19.6 0.0 reduce-scatter.2.cloned.1.call-start
  19.6 0.0 copy-done.6
  19.6 0.0 copy-done.3
  19.6 0.5 fusion.7
  20.1 0.0 copy-start.11
  20.1 0.6 copy-done.11
  20.8 0.5 convolution_bitcast_fusion
  21.3 0.1 pad.4
  21.4 0.7 copy.26
  22.0 0.0 reduce-scatter.2.cloned.1.call-update
  22.1 0.1 fusion.27
  22.2 0.1 compare_and_fusion.1
  22.2 0.6 copy-done.2
  22.9 1.9 all_gather.6
  24.8 1.0 gather_fusion
  25.8 0.0 copy-start.1
  25.8 0.1 copy.19
  26.0 0.9 copy-done.1
  26.9 0.8 gather_fusion.3
  27.7 0.9 fusion.2
  28.6 0.4 convolution_bitcast_fusion.2
  29.0 0.0 copy-start.8
  29.0 0.0 copy-start.5
  29.0 0.0 all-to-all-done
  29.0 7.0 %all-to-all-start.1 = ((f32[16,8,1024]{2,1,0:T(8,128)}), f32[16,8,1024]{2,1,0:T(8,128)S(1)}, u32[]{:S(2)}, u32[]{:S(2)}) async-start(f32[16,8,1024]{2,1,0:T(8,128)} %fusion.2), calls=%async_computation.1 | async-start | bytes 1048576 | tf_op jit(solution)/shard_map/all_to_all | solution.py:47
  36.1 0.0 all-reduce.3.cloned.1.call-start
  36.1 0.3 convolution_add_fusion.2
  36.4 0.0 copy-done.5
  36.4 0.6 fusion.40
  37.1 0.0 reduce-scatter.2.cloned.1.call-done
  37.1 1.6 convolution_multiply_fusion
  38.7 0.0 copy-start.13
  38.7 1.4 fusion.41
  40.1 0.0 copy-done.13
  40.1 0.9 fusion.20
  41.0 0.0 copy-start.7
  41.0 10.4 %all-to-all-done.1 = f32[16,8,1024]{2,1,0:T(8,128)S(1)} async-done(((f32[16,8,1024]{2,1,0:T(8,128)}), f32[16,8,1024]{2,1,0:T(8,128)S(1)}, u32[]{:S(2)}, u32[]{:S(2)}) %all-to-all-start.1) | async-done | bytes 524320 | tf_op jit(solution)/shard_map/all_to_all | solution.py:47
  51.5 0.0 copy-done.9
  51.5 1.0 fusion
  52.5 0.0 copy-done.7
  52.5 1.6 convolution_add_fusion
  54.1 0.0 all-reduce.3.cloned.1.call-update
  54.1 0.8 fusion.22
  55.0 1.9 all_gather.7
  56.9 0.1 copy.22
  57.0 1.6 gather_fusion.2
  58.6 0.2 copy.23
  58.8 0.5 convolution_bitcast_fusion.1
  59.3 1.4 convolution_add_fusion.1
  60.7 123.4 %all-reduce.3.cloned.1.call-done = (f32[128,1024]{1,0:T(8,128)}, f32[1024,172]{0,1:T(8,128)}) async-done(((f32[128,1024]{1,0:T(8,128)}, f32[1024,172]{0,1:T(8,128)}), (f32[128,1024]{1,0:T(8,128)}, f32[1024,172]{0,1:T(8,128)})) %all-reduce.3.cloned.1.call-update) | async-done | bytes 1228816 | tf_op jit(solution)/shard_map/psum | solution.py:82
  184.0 2.0 %copy.31 = f32[128,1024]{1,0:T(8,128)} copy(f32[128,1024]{1,0:T(8,128)} %get-tuple-element.8) | data formatting | bytes 1048576
  186.0 0.9 copy.32
  (13 shorter events, 0.0 us)
Async XLA Ops:
  7.2 29.9 %copy-start = (f32[1024,172]{0,1:T(8,128)S(1)}, f32[1024,172]{0,1:T(8,128)}, u32[]{:S(2)}) copy-start(f32[1024,172]{0,1:T(8,128)} %param.19) | copy-start | bytes 2113540
  7.2 0.8 copy-start.10
  8.2 0.7 copy-start.12
  9.0 10.7 %copy-start.6 = (f32[128,172]{0,1:T(8,128)S(1)}, f32[128,172]{0,1:T(8,128)}, u32[]{:S(2)}) copy-start(f32[128,172]{0,1:T(8,128)} %param.17) | copy-start | bytes 264196
  10.5 9.1 %copy-start.3 = (f32[1,4,128,128]{3,2,1,0:T(8,128)S(1)}, f32[1,4,128,128]{3,2,1,0:T(8,128)}, u32[]{:S(2)}) copy-start(f32[1,4,128,128]{3,2,1,0:T(8,128)} %param.12) | copy-start | bytes 786436
  11.2 17.8 %all-to-all-start = ((f32[16,8,128]{2,1,0:T(8,128)}), f32[16,8,128]{2,1,0:T(8,128)S(1)}, u32[]{:S(2)}, u32[]{:S(2)}) async-start(f32[16,8,128]{2,1,0:T(8,128)} %fusion.25), calls=%async_computation | async-start | bytes 131072 | tf_op jit(solution)/shard_map/all_to_all | solution.py:46
  19.6 17.5 %reduce-scatter.2.cloned.1.call-start = ((), (), s32[]{:S(2)}) async-start(), calls=%async_computation.3 | async-start | bytes 270336 | tf_op jit(solution)/shard_map/reduce_scatter | solution.py:72
  20.1 0.7 copy-start.11
  22.0 0.8 copy-start.2
  25.8 1.0 copy-start.1
  29.0 7.1 %copy-start.8 = (f32[128,128]{1,0:T(8,128)S(1)}, f32[128,128]{1,0:T(8,128)}, u32[]{:S(2)}) copy-start(f32[128,128]{1,0:T(8,128)} %param.14) | copy-start | bytes 196612
  29.0 7.4 %copy-start.5 = (f32[128,1024]{1,0:T(8,128)S(1)}, f32[128,1024]{1,0:T(8,128)}, u32[]{:S(2)}) copy-start(f32[128,1024]{1,0:T(8,128)} %param.18) | copy-start | bytes 1572868
  29.0 22.5 %all-to-all-start.1 = ((f32[16,8,1024]{2,1,0:T(8,128)}), f32[16,8,1024]{2,1,0:T(8,128)S(1)}, u32[]{:S(2)}, u32[]{:S(2)}) async-start(f32[16,8,1024]{2,1,0:T(8,128)} %fusion.2), calls=%async_computation.1 | async-start | bytes 1048576 | tf_op jit(solution)/shard_map/all_to_all | solution.py:47
  36.1 148.0 %all-reduce.3.cloned.1.call-start = ((), (), s32[]{:S(2)}) async-start(), calls=%async_computation.4 | async-start | bytes 2490368 | tf_op jit(solution)/shard_map/psum | solution.py:82
  38.7 1.4 copy-start.13
  40.1 11.3 %copy-start.9 = (f32[128,128]{1,0:T(8,128)S(1)}, f32[128,128]{1,0:T(8,128)}, u32[]{:S(2)}) copy-start(f32[128,128]{1,0:T(8,128)} %param.14) | copy-start | bytes 196612
  41.0 11.5 %copy-start.7 = (f32[128,172]{0,1:T(8,128)S(1)}, f32[128,172]{0,1:T(8,128)}, u32[]{:S(2)}) copy-start(f32[128,172]{0,1:T(8,128)} %param.17) | copy-start | bytes 264196
  184.0 2.0 %copy-start.4 = (f32[1024,172]{0,1:T(8,128)S(1)}, f32[1024,172]{0,1:T(8,128)}, u32[]{:S(2)}) copy-start(f32[1024,172]{0,1:T(8,128)} %get-tuple-element.9) | copy-start | bytes 2113540
Sparse Core Ops, SparseCore 0:
  23.2 8.9 reduce-scatter.1
  54.3 129.7 all-reduce.2
where the time goes:
time: 194 us
  waiting for transfers between devices  134 us (69%)
  starting transfers between devices  15.5 us (8%)
  between operations  14.4 us (7%)
  local copies, waits for them, and re-layouts  12.1 us (6%)
  matrix products  11.4 us (6%)
  blocking collectives  3.82 us (2%)
  other arithmetic  2.67 us (1%)
    psum x1, waiting for transfers between devices, on_device(): grad_one, grad_two = lax.psum((grad_one, grad_two), ('dom', 'row'))  123 us
    all_to_all x1, waiting for transfers between devices, on_device(): lax.all_to_all(hist_out, 'dom', split_axis=0, concat_axis=0, tiled=True)  10.4 us
    dot_general x9, matrix products, matmul(): jnp.dot(left, right, precision=HIGH, preferred_element_type=jnp.float32)  9.63 us
    all_to_all x1, starting transfers between devices, on_device(): lax.all_to_all(feat_out, 'dom', split_axis=0, concat_axis=0, tiled=True)  8.34 us
    all_to_all x1, starting transfers between devices, on_device(): lax.all_to_all(hist_out, 'dom', split_axis=0, concat_axis=0, tiled=True)  7.05 us
    unnamed x32, local copies, waits for them, and re-layouts  6.46 us
  transfers between devices with their start and end apart: 4, of which 2 were waited for; matrix products, arithmetic and copies ran while one was open for 7% of the time, Pallas kernels for 0%

commit v1 on v0

--- a/solution.py
+++ b/solution.py
@@ -79,7 +79,7 @@
     grad_two = grad_two + matmul(cross_hist.T, cotangent)
     grad_pre = matmul(back_grad, w_two.T) * slope_gate
     grad_one = matmul(layer_in.T, grad_pre)
-    grad_one, grad_two = lax.psum((grad_one, grad_two), ("dom", "row"))
+    grad_one, grad_two = lax.psum(lax.psum((grad_one, grad_two), "row"), "dom")
     return (logits, grad_one, grad_two)
 
 

time: 194 us -> 204 us (1.052)
  waiting for transfers between devices: 134 us -> 144 us
    psum x1 -> x2, waiting for transfers between devices: 123 us -> 133 us  [on_device(): grad_one, grad_two = lax.psum(lax.psum((grad_one, grad_two), 'row'), 'dom')]
  transfers between devices with their start and end apart: 4 -> 5, of which waited for: 2 -> 3; matrix products, arithmetic and copies ran while one was open for 7% -> 7% of each run, Pallas kernels for 0% -> 0%
where the time goes in v1:
time: 204 us; the launch traced here: 203 us
  waiting for transfers between devices  144 us (71%)
  starting transfers between devices  15.5 us (8%)
  between operations  14.1 us (7%)
  local copies, waits for them, and re-layouts  12.1 us (6%)
  matrix products  11.4 us (6%)
  blocking collectives  3.82 us (2%)
  other arithmetic  2.67 us (1%)
    psum x2, waiting for transfers between devices, on_device(): grad_one, grad_two = lax.psum(lax.psum((grad_one, grad_two), 'row'), 'dom')  133 us
    all_to_all x1, waiting for transfers between devices, on_device(): lax.all_to_all(hist_out, 'dom', split_axis=0, concat_axis=0, tiled=True)  10.4 us
    dot_general x9, matrix products, matmul(): jnp.dot(left, right, precision=HIGH, preferred_element_type=jnp.float32)  9.63 us
    all_to_all x1, starting transfers between devices, on_device(): lax.all_to_all(feat_out, 'dom', split_axis=0, concat_axis=0, tiled=True)  8.34 us
    all_to_all x1, starting transfers between devices, on_device(): lax.all_to_all(hist_out, 'dom', split_axis=0, concat_axis=0, tiled=True)  7.05 us
    unnamed x32, local copies, waits for them, and re-layouts  6.46 us
  transfers between devices with their start and end apart: 5, of which 3 were waited for; matrix products, arithmetic and copies ran while one was open for 7% of the time, Pallas kernels for 0%

profile of v1, /device:TPU:0, one launch (start us, length us, event | category | flops | bytes accessed | tf_op | source)
XLA Modules:
  0.0 203.1 jit_solution(9234498677462944556)
XLA Ops:
  7.2 0.0 copy-start
  7.2 0.0 copy-start.10
  7.2 0.8 compare_and_fusion
  8.0 0.0 copy-done.10
  8.0 0.1 copy.20
  8.1 0.1 copy.21
  8.1 0.1 reshape.276
  8.2 0.0 copy-start.12
  8.2 0.6 copy-done.12
  8.9 0.1 fusion.26
  9.0 1.5 gather_fusion.1
  10.5 0.7 fusion.25
  11.2 8.3 %all-to-all-start = ((f32[16,8,128]{2,1,0:T(8,128)}), f32[16,8,128]{2,1,0:T(8,128)S(1)}, u32[]{:S(2)}, u32[]{:S(2)}) async-start(f32[16,8,128]{2,1,0:T(8,128)} %fusion.25), calls=%async_computation | async-start | bytes 131072 | tf_op jit(solution)/shard_map/all_to_all | solution.py:46
  19.6 0.0 reduce-scatter.2.cloned.1.call-start
  19.6 0.0 copy-done.6
  19.6 0.0 copy-done.3
  19.6 0.5 fusion.7
  20.1 0.0 copy-start.11
  20.1 0.6 copy-done.11
  20.8 0.5 convolution_bitcast_fusion
  21.3 0.1 pad.4
  21.4 0.7 copy.26
  22.0 0.0 reduce-scatter.2.cloned.1.call-update
  22.1 0.1 fusion.27
  22.2 0.1 compare_and_fusion.1
  22.2 0.6 copy-done.2
  22.9 1.9 all_gather.6
  24.8 1.0 gather_fusion
  25.8 0.0 copy-start.1
  25.8 0.1 copy.19
  26.0 0.9 copy-done.1
  26.9 0.8 gather_fusion.3
  27.7 0.9 fusion.2
  28.6 0.4 convolution_bitcast_fusion.2
  29.0 0.0 copy-start.8
  29.0 0.0 copy-start.5
  29.0 0.0 all-to-all-done
  29.0 7.1 %all-to-all-start.1 = ((f32[16,8,1024]{2,1,0:T(8,128)}), f32[16,8,1024]{2,1,0:T(8,128)S(1)}, u32[]{:S(2)}, u32[]{:S(2)}) async-start(f32[16,8,1024]{2,1,0:T(8,128)} %fusion.2), calls=%async_computation.1 | async-start | bytes 1048576 | tf_op jit(solution)/shard_map/all_to_all | solution.py:47
  36.1 0.0 all-reduce.7.cloned.1.call-start
  36.1 0.3 convolution_add_fusion.2
  36.4 0.6 fusion.40
  37.1 0.0 reduce-scatter.2.cloned.1.call-done
  37.1 0.0 copy-done
  37.1 1.6 convolution_multiply_fusion
  38.7 1.4 fusion.41
  40.1 0.9 fusion.20
  41.0 0.0 copy-start.7
  41.0 10.4 %all-to-all-done.1 = f32[16,8,1024]{2,1,0:T(8,128)S(1)} async-done(((f32[16,8,1024]{2,1,0:T(8,128)}), f32[16,8,1024]{2,1,0:T(8,128)S(1)}, u32[]{:S(2)}, u32[]{:S(2)}) %all-to-all-start.1) | async-done | bytes 524320 | tf_op jit(solution)/shard_map/all_to_all | solution.py:47
  51.5 1.0 fusion
  52.5 1.6 convolution_add_fusion
  54.1 0.0 all-reduce.7.cloned.1.call-update
  54.1 0.0 all-reduce.5.cloned.1.call-start
  54.2 18.3 %all-reduce.7.cloned.1.call-done = (f32[128,1024]{1,0:T(8,128)}, f32[1024,172]{0,1:T(8,128)}) async-done(((f32[128,1024]{1,0:T(8,128)}, f32[1024,172]{0,1:T(8,128)}), (f32[128,1024]{1,0:T(8,128)}, f32[1024,172]{0,1:T(8,128)})) %all-reduce.7.cloned.1.call-update) | async-done | bytes 1228816 | tf_op jit(solution)/shard_map/psum | solution.py:82
  72.5 0.0 all-reduce.5.cloned.1.call-update
  72.5 0.8 fusion.22
  73.3 1.9 all_gather.7
  75.3 0.1 copy.22
  75.4 1.6 gather_fusion.2
  77.0 0.2 copy.23
  77.2 0.5 convolution_bitcast_fusion.1
  77.7 1.4 convolution_add_fusion.1
  79.0 114.7 %all-reduce.5.cloned.1.call-done = (f32[128,1024]{1,0:T(8,128)}, f32[1024,172]{0,1:T(8,128)}) async-done(((f32[128,1024]{1,0:T(8,128)}, f32[1024,172]{0,1:T(8,128)}), (f32[128,1024]{1,0:T(8,128)}, f32[1024,172]{0,1:T(8,128)})) %all-reduce.5.cloned.1.call-update) | async-done | bytes 1228816 | tf_op jit(solution)/shard_map/psum | solution.py:82
  193.8 2.0 copy.33
  195.7 0.9 copy.34
  (16 shorter events, 0.0 us)
Async XLA Ops:
  7.2 29.9 %copy-start = (f32[1024,172]{0,1:T(8,128)S(1)}, f32[1024,172]{0,1:T(8,128)}, u32[]{:S(2)}) copy-start(f32[1024,172]{0,1:T(8,128)} %param.19) | copy-start | bytes 2113540
  7.2 0.8 copy-start.10
  8.2 0.7 copy-start.12
  9.0 10.7 %copy-start.6 = (f32[128,172]{0,1:T(8,128)S(1)}, f32[128,172]{0,1:T(8,128)}, u32[]{:S(2)}) copy-start(f32[128,172]{0,1:T(8,128)} %param.17) | copy-start | bytes 264196
  10.5 9.2 %copy-start.3 = (f32[1,4,128,128]{3,2,1,0:T(8,128)S(1)}, f32[1,4,128,128]{3,2,1,0:T(8,128)}, u32[]{:S(2)}) copy-start(f32[1,4,128,128]{3,2,1,0:T(8,128)} %param.12) | copy-start | bytes 786436
  11.2 17.8 %all-to-all-start = ((f32[16,8,128]{2,1,0:T(8,128)}), f32[16,8,128]{2,1,0:T(8,128)S(1)}, u32[]{:S(2)}, u32[]{:S(2)}) async-start(f32[16,8,128]{2,1,0:T(8,128)} %fusion.25), calls=%async_computation | async-start | bytes 131072 | tf_op jit(solution)/shard_map/all_to_all | solution.py:46
  19.6 17.5 %reduce-scatter.2.cloned.1.call-start = ((), (), s32[]{:S(2)}) async-start(), calls=%async_computation.3 | async-start | bytes 270336 | tf_op jit(solution)/shard_map/reduce_scatter | solution.py:72
  20.1 0.7 copy-start.11
  22.0 0.8 copy-start.2
  25.8 1.0 copy-start.1
  29.0 7.1 %copy-start.8 = (f32[128,128]{1,0:T(8,128)S(1)}, f32[128,128]{1,0:T(8,128)}, u32[]{:S(2)}) copy-start(f32[128,128]{1,0:T(8,128)} %param.14) | copy-start | bytes 196612
  29.0 7.4 %copy-start.5 = (f32[128,1024]{1,0:T(8,128)S(1)}, f32[128,1024]{1,0:T(8,128)}, u32[]{:S(2)}) copy-start(f32[128,1024]{1,0:T(8,128)} %param.18) | copy-start | bytes 1572868
  29.0 22.5 %all-to-all-start.1 = ((f32[16,8,1024]{2,1,0:T(8,128)}), f32[16,8,1024]{2,1,0:T(8,128)S(1)}, u32[]{:S(2)}, u32[]{:S(2)}) async-start(f32[16,8,1024]{2,1,0:T(8,128)} %fusion.2), calls=%async_computation.1 | async-start | bytes 1048576 | tf_op jit(solution)/shard_map/all_to_all | solution.py:47
  36.1 36.4 %all-reduce.7.cloned.1.call-start = ((), (), s32[]{:S(2)}) async-start(), calls=%async_computation.5 | async-start | bytes 2490368 | tf_op jit(solution)/shard_map/psum | solution.py:82
  38.7 1.4 copy-start.13
  40.1 11.3 %copy-start.9 = (f32[128,128]{1,0:T(8,128)S(1)}, f32[128,128]{1,0:T(8,128)}, u32[]{:S(2)}) copy-start(f32[128,128]{1,0:T(8,128)} %param.14) | copy-start | bytes 196612
  41.0 11.5 %copy-start.7 = (f32[128,172]{0,1:T(8,128)S(1)}, f32[128,172]{0,1:T(8,128)}, u32[]{:S(2)}) copy-start(f32[128,172]{0,1:T(8,128)} %param.17) | copy-start | bytes 264196
  54.1 139.7 %all-reduce.5.cloned.1.call-start = ((), (), s32[]{:S(2)}) async-start(), calls=%async_computation.4 | async-start | bytes 2490368 | tf_op jit(solution)/shard_map/psum | solution.py:82
  193.8 2.0 copy-start.4
Sparse Core Ops, SparseCore 0:
  23.2 8.9 reduce-scatter.1
  54.2 18.1 all-reduce.6
  78.1 115.6 all-reduce.4
